TPU v7x, 1024 devices: a whole 4x8x16 slice. The times are simulated.
1024 devices in a mesh: dom: 8 (over y_lo, core), band: 128 (over y_hi, z, x).
Axes of the slice: x: 4, y: 8 (y_hi: 2, y_lo: 4; y = y_hi * 4 + y_lo), z: 16, core: 2. Of those that a mesh axis runs over, the one named last changes fastest.
Arguments:
- psi_in: float32 [8, 128, 20, 1600], P('dom', 'band'), may hold values from -6 to 6
- v_in: float32 [8, 40, 1600], P('dom'), may hold values from -3 to 3
- offsets: int32 [8, 3], replicated, may hold values from 0 to 32, as said below
Outputs:
- psi_out: float32 [8, 128, 20, 1600], P('dom', 'band')
Inputs may be any that keep to these rules, and one draw needn't show every extreme that they name: `offsets`: row d is the first corner of domain d's core in the global grid: its first two entries are 0 or 32, its third a multiple of 32 below 64; the 8 rows are distinct, so the cores tile the grid.
All inputs are finite; a program needn't handle non-finite values.
Results may differ from a plain program's by a relative error of at most 0.0003.
Values sent between devices are 32-bit elements; how exact they have to be, the bound alone decides.
A program may use at most 64 MiB of HBM per device.

v0:
```python
import math

import jax
import jax.numpy as jnp
from jax import lax
from jax.sharding import Mesh
from jax.sharding import PartitionSpec as P

CORE = 32
BUF = 4
DEG = 8
BAND = ("band_0", "band_1", "band_2")


CENTER = 3.0
HALF_WIDTH = 4.5
FOUR_PI = 4.0 * math.pi
EXCHANGE_COEF = -((3.0 / math.pi) ** (1.0 / 3.0))
precise = lax.Precision.HIGHEST


def swapped(value, axis, distance):
    mask = 2**distance
    pairs = [(source, source ^ mask) for source in range(lax.axis_size(axis))]
    return lax.ppermute(value, axis, pairs)


def reduced_to_own(parts, axes, sequence):
    inside = parts.shape[1:]
    parts = parts.reshape(*(lax.axis_size(a) for a in axes), *inside)
    parts = jnp.moveaxis(parts, sequence, range(len(axes))).reshape(-1, *inside)
    for k in sequence:
        parts = lax.psum_scatter(parts, axes[k], scatter_dimension=0, tiled=True)
    return parts[0]


def split_up(value, dim, peers):
    before, after = (value.shape[:dim], value.shape[dim + 1 :])
    return jnp.moveaxis(value.reshape(*before, peers, -1, *after), dim, 0)


def sum_by_axis(value, axes, sequence, dim):
    peers = lax.axis_size(axes)
    return reduced_to_own(split_up(value, dim, peers), axes, sequence)


def copy_for_each(value, axis):
    copies = jnp.broadcast_to(value, (lax.axis_size(axis), *value.shape))
    return lax.all_to_all(copies, axis, split_axis=0, concat_axis=0, tiled=True)


def of_everyone(value, axis):
    everything = copy_for_each(value, axis)
    return jnp.sum(everything, axis=0)


def in_one_piece(arrays, axis, dim, along):
    both = jnp.concatenate(arrays, axis=along)
    out, at, done = (lax.all_gather(both, axis, axis=dim, tiled=True), 0, [])
    for a in arrays:
        done.append(lax.slice_in_dim(out, at, at + a.shape[along], axis=along))
        at += a.shape[along]
    return tuple(done)


def hamiltonian(values, potential, lower_slab, side_len):
    row_len = values.shape[1]
    zero_row = jnp.zeros((1, row_len), jnp.float32)
    face_row = jnp.where(lower_slab, values[-1:], values[:1])
    partner_row = swapped(face_row, BAND, 0)
    prev_fill = jnp.where(lower_slab, zero_row, partner_row)
    next_fill = jnp.where(lower_slab, partner_row, zero_row)
    prev_rows = jnp.concatenate([prev_fill, values[:-1]], 0)
    next_rows = jnp.concatenate([values[1:], next_fill], 0)
    column = jnp.arange(row_len) % side_len
    prev_cols = jnp.where(column == 0, 0.0, jnp.roll(values, 1, 1))
    next_cols = jnp.where(column == side_len - 1, 0.0, jnp.roll(values, -1, 1))
    zero_block = jnp.zeros((values.shape[0], side_len), jnp.float32)
    prev_lines = jnp.concatenate([zero_block, values[:, :-side_len]], 1)
    next_lines = jnp.concatenate([values[:, side_len:], zero_block], 1)
    beside_all = prev_rows + next_rows + prev_lines + next_lines + prev_cols + next_cols
    return 0.5 * (6.0 * values - beside_all) + potential * values


def chebyshev(values, potential, lower_slab, side_len):

    def shifted(operand):
        return (
            hamiltonian(operand, potential, lower_slab, side_len) - CENTER * operand
        ) / HALF_WIDTH

    previous = values
    current = shifted(values)
    for order_idx in range(DEG - 1):
        following = 2.0 * shifted(current) - previous
        previous, current = (current, following)
    return current


def phase_tables(positions, freqs, length):
    product = positions[..., None] * freqs % length
    angle = 2.0 * math.pi / length * product.astype(jnp.float32)
    return (jnp.cos(angle), jnp.sin(angle))


def poisson_factor(depth_waves, grid_z):
    wave_x = jnp.arange(2 * CORE, dtype=jnp.int32)
    eigen_x = 2.0 - 2.0 * jnp.cos(2.0 * math.pi * wave_x.astype(jnp.float32) / (2 * CORE))
    eigen_z = 2.0 - 2.0 * jnp.cos(2.0 * math.pi * depth_waves.astype(jnp.float32) / grid_z)
    eigen = eigen_z[:, None, None] + eigen_x[None, :, None] + eigen_x[None, None, :]
    zero_mode = (
        (depth_waves == 0)[:, None, None]
        & (wave_x == 0)[None, :, None]
        & (wave_x == 0)[None, None, :]
    )
    return jnp.where(zero_mode, 0.0, FOUR_PI / jnp.where(zero_mode, 1.0, eigen))


def plane_spectrum(own_parts, first_part, anchor):
    part_count = own_parts.shape[0]
    cell_ids = jnp.arange(CORE, dtype=jnp.int32)
    wave_ids = jnp.arange(2 * CORE, dtype=jnp.int32)
    cos_x, sin_x = phase_tables(anchor[0] + cell_ids, wave_ids, 2 * CORE)
    cos_y, sin_y = phase_tables(anchor[1] + cell_ids, wave_ids, 2 * CORE)
    with_cos = jnp.einsum("txy,yk->txk", own_parts, cos_y, precision=precise)
    with_sin = jnp.einsum("txy,yk->txk", own_parts, sin_y, precision=precise)
    real_part = jnp.einsum("xj,txk->tjk", cos_x, with_cos, precision=precise) - jnp.einsum(
        "xj,txk->tjk", sin_x, with_sin, precision=precise
    )
    imag_part = -(
        jnp.einsum("xj,txk->tjk", sin_x, with_cos, precision=precise)
        + jnp.einsum("xj,txk->tjk", cos_x, with_sin, precision=precise)
    )
    odd_part = ((first_part + jnp.arange(part_count, dtype=jnp.int32)) % 2 == 1)[:, None, None]
    return jnp.stack(
        [jnp.where(odd_part, -imag_part, real_part), jnp.where(odd_part, real_part, imag_part)], 1
    )


def field_planes(all_spectra, first_part, anchor, side_len, grid_z):
    part_count = all_spectra.shape[0]
    depth_waves = (first_part + jnp.arange(part_count, dtype=jnp.int32)) // 2
    factor = poisson_factor(depth_waves, grid_z)
    real_in = jnp.stack([all_spectra[:, 0], all_spectra[:, 0] * factor], 1)
    imag_in = jnp.stack([all_spectra[:, 1], all_spectra[:, 1] * factor], 1)
    wave_ids = jnp.arange(2 * CORE, dtype=jnp.int32)
    region_pos = jnp.arange(side_len, dtype=jnp.int32) - BUF
    cos_x, sin_x = phase_tables(anchor[0] + region_pos, wave_ids, 2 * CORE)
    cos_y, sin_y = phase_tables(anchor[1] + region_pos, wave_ids, 2 * CORE)
    first_re = jnp.einsum("tfjk,rj->tfrk", real_in, cos_x, precision=precise) - jnp.einsum(
        "tfjk,rj->tfrk", imag_in, sin_x, precision=precise
    )
    first_im = jnp.einsum("tfjk,rj->tfrk", real_in, sin_x, precision=precise) + jnp.einsum(
        "tfjk,rj->tfrk", imag_in, cos_x, precision=precise
    )
    plane_re = jnp.einsum("tfrk,sk->tfrs", first_re, cos_y, precision=precise) - jnp.einsum(
        "tfrk,sk->tfrs", first_im, sin_y, precision=precise
    )
    plane_im = jnp.einsum("tfrk,sk->tfrs", first_re, sin_y, precision=precise) + jnp.einsum(
        "tfrk,sk->tfrs", first_im, cos_y, precision=precise
    )
    return (plane_re, plane_im)


def depth_terms(plane_re, plane_im, anchor_z, side_len, grid_z):
    part_count = plane_re.shape[0]
    depth_waves = jnp.arange(part_count, dtype=jnp.int32) // 2
    region_pos = jnp.arange(side_len, dtype=jnp.int32) - BUF
    cos_z, sin_z = phase_tables(anchor_z + region_pos, depth_waves, grid_z)
    return jnp.einsum("tfxy,zt->fxyz", plane_re, cos_z, precision=precise) - jnp.einsum(
        "tfxy,zt->fxyz", plane_im, sin_z, precision=precise
    )


def local(psi_in, v_in, offsets):
    band_count = lax.axis_size(BAND)
    dom_count = lax.axis_size("dom")
    band_idx = lax.axis_index(BAND)
    dom_idx = lax.axis_index("dom")
    slab_idx = band_idx % 2
    lower_slab = slab_idx == 0
    side_len = v_in.shape[1]
    half_rows = side_len // 2
    grid_z = CORE * dom_count // 4
    cell_count = 4 * CORE * CORE * grid_z
    wavefunc = psi_in[0, 0]
    row_start = slab_idx * half_rows
    potential_in = lax.dynamic_slice_in_dim(v_in[0], row_start, half_rows, 0)
    filtered = chebyshev(wavefunc, potential_in, lower_slab, side_len)
    anchor = lax.dynamic_slice_in_dim(offsets, dom_idx, 1, 0)[0]
    slab_cube = filtered.reshape(half_rows, side_len, side_len)
    core_rows = lax.dynamic_slice_in_dim(slab_cube, jnp.where(lower_slab, BUF, 0), CORE // 2, 0)
    squares = core_rows[:, BUF : BUF + CORE, BUF : BUF + CORE] ** 2 / (band_count // 2)
    density = lax.dynamic_update_slice_in_dim(
        jnp.zeros((CORE, CORE, CORE), jnp.float32), squares, slab_idx * (CORE // 2), 0
    )
    cos_z, sin_z = phase_tables(
        anchor[2] + jnp.arange(CORE, dtype=jnp.int32), jnp.arange(grid_z, dtype=jnp.int32), grid_z
    )
    z_table = jnp.stack([cos_z, -sin_z], 2).reshape(CORE, 2 * grid_z)
    zparts = jnp.einsum("xyz,zq->qxy", density, z_table, precision=precise)
    own_parts = sum_by_axis(zparts, BAND, (2, 1, 0), 0)
    first_part = band_idx * own_parts.shape[0]
    spectrum = plane_spectrum(own_parts, first_part, anchor)
    all_spectra = of_everyone(spectrum, "dom")
    plane_re, plane_im = field_planes(all_spectra, first_part, anchor, side_len, grid_z)
    every_re, every_im = in_one_piece((plane_re, plane_im), BAND, 0, 1)
    slab_re = lax.dynamic_slice_in_dim(every_re, row_start, half_rows, 2)
    slab_im = lax.dynamic_slice_in_dim(every_im, row_start, half_rows, 2)
    fields = depth_terms(slab_re, slab_im, anchor[2], side_len, grid_z)
    fields = fields / cell_count
    density_rows = fields[0].reshape(half_rows, side_len * side_len)
    hartree_rows = fields[1].reshape(half_rows, side_len * side_len)
    renewed = potential_in + hartree_rows + EXCHANGE_COEF * jnp.cbrt(density_rows)
    result = chebyshev(filtered, renewed, lower_slab, side_len)
    return result[None, None]


def solution(mesh):
    split = Mesh(
        mesh.devices.reshape(mesh.shape["dom"], 2, 16, 4), ("dom", "band_0", "band_1", "band_2")
    )
    return jax.shard_map(
        local,
        mesh=split,
        in_specs=(P("dom", BAND, None, None), P("dom", None, None), P()),
        out_specs=P("dom", BAND, None, None),
        check_vma=False,
    )
```

profile of v0, /device:TPU:4, one launch (start us, length us, event | category | flops | bytes accessed | tf_op | source)
XLA Modules:
  0.0 600.8 jit_solution(17986319086056781482)
XLA Ops:
  7.3 3.1 collective-permute-start
  14.8 2.7 collective-permute-start.1
  17.7 2.7 collective-permute-done.1
  20.9 2.7 collective-permute-start.2
  23.7 2.7 collective-permute-done.2
  26.9 2.7 collective-permute-start.3
  29.7 2.7 collective-permute-done.3
  32.9 2.7 collective-permute-start.4
  35.8 2.8 collective-permute-done.4
  39.0 2.7 collective-permute-start.5
  41.8 2.7 collective-permute-done.5
  45.0 2.7 collective-permute-start.6
  47.9 2.7 collective-permute-done.6
  51.1 2.7 collective-permute-start.7
  53.9 2.7 collective-permute-done.7
  61.8 46.7 %reduce-scatter.4.cloned.1.call-done = f32[32,1,32,32]{3,2,0,1:T(8,128)} async-done(((f32[128,1,32,32]{3,2,0,1:T(8,128)}), f32[32,1,32,32]{3,2,0,1:T(8,128)}) %reduce-scatter.4.cloned.1.call-update) | async-done | bytes 131088 | tf_op jit(solution)/shard_map/reduce_scatter | solution.py:33
  109.2 78.5 %reduce-scatter.6.cloned.1.call-done = f32[2,1,32,32]{3,2,0,1:T(8,128)} async-done(((f32[32,1,32,32]{3,2,0,1:T(8,128)}), f32[2,1,32,32]{3,2,0,1:T(8,128)}) %reduce-scatter.6.cloned.1.call-update) | async-done | bytes 8208 | tf_op jit(solution)/shard_map/reduce_scatter | solution.py:33
  188.2 26.8 %reduce-scatter.8.cloned.1.call-done = f32[1,1,32,32]{3,2,0,1:T(8,128)} async-done(((f32[2,1,32,32]{3,2,0,1:T(8,128)}), f32[1,1,32,32]{3,2,0,1:T(8,128)}) %reduce-scatter.8.cloned.1.call-update) | async-done | bytes 4112 | tf_op jit(solution)/shard_map/reduce_scatter | solution.py:33
  219.5 3.4 all-to-all-start
  224.2 8.3 %all-to-all-done = f32[8,1,8192]{2,1,0:T(1,128)S(1)} async-done(((f32[8,1,8192]{2,1,0:T(1,128)}), f32[8,1,8192]{2,1,0:T(1,128)S(1)}, u32[]{:S(2)}, u32[]{:S(2)}) %all-to-all-start) | async-done | bytes 262176 | tf_op jit(solution)/shard_map/all_to_all | solution.py:49
  238.7 3.3 collective-permute-start.8
  244.2 291.8 %all-gather.2.cloned.1.call-done = f32[128,4,40,40]{3,2,1,0:T(8,128)} async-done(((f32[1,4,40,40]{3,2,1,0:T(8,128)}), f32[128,4,40,40]{3,2,1,0:T(8,128)}) %all-gather.2.cloned.1.call-update) | async-done | bytes 3276816 | tf_op jit(solution)/shard_map/all_gather | solution.py:59
  536.0 4.8 fusion.341
  541.5 4.5 fusion
  545.9 4.5 fusion.7
  551.6 2.9 collective-permute-start.9
  557.6 2.9 collective-permute-start.10
  563.7 2.9 collective-permute-start.11
  569.7 2.9 collective-permute-start.12
  575.7 2.9 collective-permute-start.13
  581.8 2.9 collective-permute-start.14
  587.8 2.9 collective-permute-start.15
  (187 shorter events, 52.6 us)
Async XLA Ops:
  6.5 6.2 %copy-start = (s32[8,3]{0,1:T(4,128)S(1)}, s32[8,3]{0,1:T(4,128)}, u32[]{:S(2)}) copy-start(s32[8,3]{0,1:T(4,128)} %param.5) | copy-start | bytes 292
  6.5 7.8 %copy-start.2 = (f32[1,1,20,1600]{3,1,2,0:T(1,128)S(1)}, f32[1,1,20,1600]{3,1,2,0:T(1,128)}, u32[]{:S(2)}) copy-start(f32[1,1,20,1600]{3,1,2,0:T(1,128)} %param.3) | copy-start | bytes 384004
  6.5 7.8 %copy-start.1 = (f32[1,40,1600]{2,1,0:T(8,128)S(1)}, f32[1,40,1600]{2,1,0:T(8,128)}, u32[]{:S(2)}) copy-start(f32[1,40,1600]{2,1,0:T(8,128)} %param.4) | copy-start | bytes 768004
  6.5 102.0 %reduce-scatter.4.cloned.1.call-start = ((), (), s32[]{:S(2)}) async-start(), calls=%async_computation.4 | async-start | bytes 2621440 | tf_op jit(solution)/shard_map/reduce_scatter | solution.py:33
  7.3 7.0 %collective-permute-start = (f32[1,1600]{1,0:T(1,128)S(1)}, f32[1,1600]{1,0:T(1,128)S(1)}, u32[]{:S(2)}, u32[]{:S(2)}) collective-permute-start(f32[1,1600]{1,0:T(1,128)S(1)} %fusion.266), channel_id=1, source_target_pairs={{0,1},{1,0},{2,3},{3,2},{4,5},{5,4},{6,7},{7,6},{8,9},{9,8},{10,11... | collective-permute-start | bytes 19208 | tf_op jit(solution)/shard_map/ppermute | solution.py:25
  14.8 5.5 collective-permute-start.1
  20.9 5.5 collective-permute-start.2
  26.9 5.5 collective-permute-start.3
  32.9 5.6 collective-permute-start.4
  39.0 5.5 collective-permute-start.5
  45.0 5.5 collective-permute-start.6
  51.1 5.5 collective-permute-start.7
  61.8 125.8 %reduce-scatter.6.cloned.1.call-start = ((), (), s32[]{:S(2)}) async-start(), calls=%async_computation.5 | async-start | bytes 557056 | tf_op jit(solution)/shard_map/reduce_scatter | solution.py:33
  108.6 106.5 %reduce-scatter.8.cloned.1.call-start = ((), (), s32[]{:S(2)}) async-start(), calls=%async_computation.6 | async-start | bytes 49152 | tf_op jit(solution)/shard_map/reduce_scatter | solution.py:33
  219.5 13.1 %all-to-all-start = ((f32[8,1,8192]{2,1,0:T(1,128)}), f32[8,1,8192]{2,1,0:T(1,128)S(1)}, u32[]{:S(2)}, u32[]{:S(2)}) async-start(f32[8,1,8192]{2,1,0:T(1,128)} %reshape.469), calls=%async_computation.3 | async-start | bytes 524288 | tf_op jit(solution)/shard_map/all_to_all | solution.py:49
  222.9 313.1 %all-gather.2.cloned.1.call-start = ((), (), s32[]{:S(2)}) async-start(), calls=%async_computation.7 | async-start | bytes 10567680 | tf_op jit(solution)/shard_map/all_gather | solution.py:59
  238.7 5.5 collective-permute-start.8
  551.6 5.5 collective-permute-start.9
  557.6 5.5 collective-permute-start.10
  563.7 5.5 collective-permute-start.11
  569.7 5.5 collective-permute-start.12
  575.7 5.5 collective-permute-start.13
  581.8 5.5 collective-permute-start.14
  587.8 5.5 collective-permute-start.15
Sparse Core Ops, SparseCore 0:
  61.9 46.5 reduce-scatter.3
  111.9 75.7 reduce-scatter.5
  191.0 24.0 reduce-scatter.7
  238.1 297.8 all-gather.1
where the time goes:
time: 602 us; the launch traced here: 601 us
  waiting for transfers between devices  491 us (82%)
  starting transfers between devices  49.2 us (8%)
  local copies, waits for them, and re-layouts  18.1 us (3%)
  matrix products  17.3 us (3%)
  between operations  14.4 us (2%)
  other arithmetic  10.8 us (2%)
    all_gather x1, waiting for transfers between devices, in_one_piece(): out, at, done = (lax.all_gather(both, axis, axis=dim, tiled=True), 0, [])  292 us
    reduce_scatter x3, waiting for transfers between devices, reduced_to_own(): parts = lax.psum_scatter(parts, axes[k], scatter_dimension=0, tiled=True)  152 us
    ppermute x16, starting transfers between devices, swapped(): return lax.ppermute(value, axis, pairs)  45.7 us
    ppermute x16, waiting for transfers between devices, swapped(): return lax.ppermute(value, axis, pairs)  39 us
  transfers between devices with their start and end apart: 21, of which 20 were waited for; matrix products, arithmetic and copies ran while one was open for 1% of the time, Pallas kernels for 0%

commit v1 on v0

v1 whole, which is shorter than its diff:
```python
import functools
import math

import jax
import jax.numpy as jnp
import numpy as np
from jax import lax
from jax.experimental import pallas as pl
from jax.experimental.pallas import tpu as pltpu
from jax.sharding import PartitionSpec as P

F32 = jnp.float32
MESH = pl.DeviceIdType.MESH
GRID = 64
SIDE = 40
BUF = 4
LANE = 128
GAP = 42
ROWS = 10
SLOTS = 28
HALO = 8
DEG = 8
HALF_WIDTH = 4.5
EXCHANGE = -((3.0 / math.pi) ** (1.0 / 3.0))
PART = 24


def wave_list():
    even = [("c", k) for k in range(0, 33, 2)] + [("s", k) for k in range(2, 32, 2)]
    odd = [("c", k) for k in range(1, 32, 2)] + [("s", k) for k in range(1, 32, 2)]
    return even + odd


def basis(cells):
    cells = np.asarray(cells, np.float64)
    rows = []
    for kind, k in wave_list():
        angle = 2.0 * np.pi * k * cells / GRID
        size = 1.0 if k in (0, 32) else 2.0
        rows.append(np.sqrt(size / GRID) * (np.cos(angle) if kind == "c" else np.sin(angle)))
    return np.stack(rows)


def tables():
    waves = np.array([k for _, k in wave_list()])
    lam = 2.0 - 2.0 * np.cos(2.0 * np.pi * waves / GRID)
    by = basis(np.arange(32))
    cz = np.tile(basis(np.arange(32)).T, (4, 2))
    cx = np.zeros((GRID, 4, 8, 2, 4))
    for q in range(4):
        for s in range(2):
            for t in range(4):
                n = 4 * t + q
                cx[:, q, :, s, t] = basis([n if s == 0 else 31 - n])
    cx = cx.reshape(GRID, 256)
    xall = np.zeros((3, 2, 2, ROWS, GRID))
    for g in range(3):
        for s in range(2):
            for r in range(ROWS):
                slot = ROWS * g + r
                if slot < SLOTS:
                    wave = basis([slot - BUF if s == 0 else 35 - slot])[:, 0]
                    xall[g, 0, s, r, :32] = wave[:32]
                    xall[g, 1, s, r, 32:] = wave[32:]
    xall = xall.reshape(120, GRID)
    zt = np.zeros((256, 2, LANE))
    region = basis(np.arange(SIDE) - BUF)
    for g in range(3):
        for b in range(2):
            zt[64 * g + 32 * b : 64 * g + 32 * b + 32, b, GAP * g : GAP * g + SIDE] = region[
                32 * b : 32 * b + 32
            ]
    zt = zt.reshape(256, 256)
    yt = region.T
    lam2 = np.concatenate(
        [lam[:32, None] + lam[None, :], lam[32:, None] + lam[None, :]], axis=1
    )
    out = (lam2, by, cz, cx, xall, zt, yt)
    return [np.asarray(a, np.float32) for a in out], np.asarray(lam, np.float32)


def lanes(shape):
    return lax.broadcasted_iota(jnp.int32, shape, len(shape) - 1)


def dot(a, b):
    return jnp.dot(a, b, precision=lax.Precision.HIGHEST, preferred_element_type=F32)


def roll(v, shift):
    shift %= LANE
    return v if shift == 0 else pltpu.roll(v, shift, 1)


def cbrt(x):
    a = jnp.abs(x)
    tiny = 1.2e-38
    b = jnp.maximum(a, tiny)
    y = jnp.exp(jnp.log(b) * (1.0 / 3.0))
    y = y - (y - b / (y * y)) * (1.0 / 3.0)
    y = jnp.where(a < tiny, 0.0, y)
    return jnp.where(x < 0.0, -y, y)


def line_of(ref, rows, y):
    block, at = divmod(SIDE * y, LANE)
    v = roll(ref[0:rows, block * LANE : (block + 1) * LANE], -at)
    if at + SIDE > LANE:
        w = roll(ref[0:rows, (block + 1) * LANE : (block + 2) * LANE], -at)
        v = jnp.where(lanes(v.shape) < LANE - at, v, w)
    return v


def to_tiles(ref, stride, row_of, tile):
    lane = lanes((SIDE, LANE))
    acc = jnp.zeros((SIDE, LANE), F32)
    for g in range(3):
        slot = ROWS * g + tile
        if slot < SLOTS:
            v = roll(ref[pl.ds(row_of(slot), SIDE, stride=stride), :], GAP * g)
            inside = (lane >= GAP * g) & (lane < GAP * g + SIDE)
            acc = jnp.where(inside, v, acc)
    return acc


def filter_step(src, dst, coef, first):
    lane = lanes((SIDE, LANE))
    inside = (lane < 3 * GAP) & (lane % GAP < SIDE)
    scale = (0.5 if first else 1.0) / HALF_WIDTH
    beta = jnp.where(inside, scale, 0.0).astype(F32)
    for r in range(ROWS):
        c = src[r, 8:48, :]
        if r == 0:
            below = jnp.where(lane >= GAP, roll(src[ROWS - 1, 8:48, :], GAP), 0.0)
        else:
            below = src[r - 1, 8:48, :]
        if r == ROWS - 1:
            above = roll(src[0, 8:48, :], -GAP)
        else:
            above = src[r + 1, 8:48, :]
        near = (below + above) + (src[r, 7:47, :] + src[r, 9:49, :])
        near = near + (roll(c, 1) + roll(c, -1))
        if first:
            dst[r, 8:48, :] = (0.5 * coef[r]) * c - beta * near
        else:
            dst[r, 8:48, :] = coef[r] * c - beta * near - dst[r, 8:48, :]


def chebyshev(buf_a, buf_b, coef):
    filter_step(buf_a, buf_b, coef, True)
    filter_step(buf_b, buf_a, coef, False)

    def two(_, carry):
        filter_step(buf_a, buf_b, coef, False)
        filter_step(buf_b, buf_a, coef, False)
        return carry

    lax.fori_loop(0, (DEG - 2) // 2, two, 0)


def clear_edges(buf):
    zero = jnp.zeros((8, LANE), F32)
    for r in range(ROWS):
        buf[r, 0:8, :] = zero
        buf[r, 48:56, :] = zero


def place():
    dom = lax.axis_index("dom")
    band = lax.axis_index("band")
    xi = lax.rem(band, 4)
    zi = lax.rem(band // 4, 16)
    yh = band // 64
    return dom, band, xi, zi, yh


def main_kernel(
    offs, lam_y, psi, pot, lam2, by, cz, cx, xall, zt, yt,
    field, coef_out,
    psi_pad, pot_pad, lines, pot_lines, h_send, h_recv, buf_a, buf_b, coef, squares,
    p_send, x_recv, y_send, y_recv, z_send, z_recv, z_all, r2_ref, c_send, c_recv, f_recv, h2_recv,
    h_sems, h2_sems, xs, xr, ys, yr, zs, zr, as_, ar, cs, cr, fs, fr,
):
    dom, band, xi, zi, yh = place()
    yc = yh * 8 + dom
    s = lax.rem(xi, 2)
    partner = xi + 1 - 2 * s

    def at_x(x):
        return (dom, band - xi + x)

    def at_z(z):
        return (dom, yh * 64 + z * 4 + xi)

    def at_y(c):
        return (lax.rem(c, 8), (c // 8) * 64 + zi * 4 + xi)

    def turn(value, n):
        return lax.rem(value + n, n)

    barrier = pltpu.get_barrier_semaphore()
    for o in range(1, 4):
        pl.semaphore_signal(barrier, inc=1, device_id=at_x(turn(xi + o, 4)), device_id_type=MESH)

    def greet(o, carry):
        pl.semaphore_signal(barrier, inc=1, device_id=at_z(turn(zi + o, 16)), device_id_type=MESH)
        pl.semaphore_signal(barrier, inc=1, device_id=at_y(turn(yc + o, 16)), device_id_type=MESH)
        return carry

    lax.fori_loop(1, 16, greet, 0)

    upper = s.astype(F32)
    h_send[:, 0:1600] = psi[12:20, :] * (1.0 - upper) + psi[0:8, :] * upper
    psi_pad[0:20, 0:1600] = psi[...]
    pot_pad[:, 0:1600] = pot[...]
    for y in range(SIDE):
        lines[y * 32 + 8 : y * 32 + 32, :] = line_of(psi_pad, 24, y)
    for y in range(SIDE):
        pot_lines[y * 40 : y * 40 + 40, :] = line_of(pot_pad, 40, y)
    clear_edges(buf_a)
    clear_edges(buf_b)
    for r in range(ROWS):
        coef[r] = to_tiles(
            pot_lines, 40, lambda slot: slot + s * (39 - 2 * slot), r
        ) * (2.0 / HALF_WIDTH)

    pl.semaphore_wait(barrier, 33)

    halo = pltpu.make_async_remote_copy(
        src_ref=h_send, dst_ref=h_recv, send_sem=h_sems.at[0], recv_sem=h_sems.at[1],
        device_id=at_x(partner), device_id_type=MESH,
    )
    halo.start()
    halo.wait()
    for y in range(SIDE):
        lines[y * 32 : y * 32 + 8, :] = line_of(h_recv, 8, y)

    def row_of(slot):
        if slot < 20:
            return 8 + slot + s * (19 - 2 * slot)
        return (slot - 20) + s * (47 - 2 * slot)

    for r in range(ROWS):
        buf_a[r, 8:48, :] = to_tiles(lines, 32, row_of, r)
    chebyshev(buf_a, buf_b, coef)

    lane32 = lanes((32, LANE))
    for t in range(4):
        acc = jnp.zeros((32, LANE), F32)
        for q in range(4):
            g, r = divmod(BUF + 4 * t + q, ROWS)
            v = roll(buf_a[r, 12:44, :], 32 * q - GAP * g - BUF)
            acc = jnp.where(lane32 // 32 == q, v, acc)
        squares[:, t * LANE : (t + 1) * LANE] = acc * acc * (1.0 / 64.0)

    def sign(d, axis):
        return 1.0 - offs[d, axis].astype(F32) * (1.0 / 16.0)

    sign_y = sign(dom, 1)
    odd_row = lax.broadcasted_iota(jnp.int32, (GRID, 32), 0) >= 32
    parts = dot(jnp.where(odd_row, sign_y, 1.0) * by[...], squares[...])
    for x in range(4):
        p_send[x] = parts[16 * x : 16 * x + 16]

    def x_copy(x, slot):
        return pltpu.make_async_remote_copy(
            src_ref=p_send.at[x], dst_ref=x_recv.at[slot], send_sem=xs.at[x],
            recv_sem=xr.at[slot], device_id=at_x(x), device_id_type=MESH,
        )

    for o in (2, 1, 3):
        x_copy(turn(xi + o, 4), xi).start()
    x_recv[xi] = p_send[xi]
    halo2 = pltpu.make_async_remote_copy(
        src_ref=buf_a.at[2:10, 8:48, :], dst_ref=h2_recv, send_sem=h2_sems.at[0],
        recv_sem=h2_sems.at[1], device_id=at_x(partner), device_id_type=MESH,
    )
    halo2.start()
    for o in (1, 3, 2):
        x_copy(turn(xi + o, 4), turn(xi - o + 4, 4)).wait_recv()
    for h in range(2):
        both = x_recv[h] + x_recv[h + 2]
        for t in range(4):
            y_send[pl.ds(h * 4 + t, 16, stride=8), :] = both[:, t * LANE : (t + 1) * LANE]

    def rows(index, size):
        return pl.ds(pl.multiple_of(index * size, 8), size)

    def y_copy(c, slot):
        return pltpu.make_async_remote_copy(
            src_ref=y_send.at[rows(c, 8)], dst_ref=y_recv.at[rows(slot, 8)], send_sem=ys.at[c],
            recv_sem=yr.at[slot], device_id=at_y(c), device_id_type=MESH,
        )

    def y_start(o, carry):
        y_copy(turn(yc + o, 16), yc).start()
        return carry

    def y_wait(o, carry):
        y_copy(turn(yc + o, 16), turn(yc - o + 16, 16)).wait_recv()
        return carry

    lax.fori_loop(1, 16, y_start, 0)
    y_recv[rows(yc, 8), :] = y_send[rows(yc, 8), :]
    lax.fori_loop(1, 16, y_wait, 0)

    d_all = y_recv[0:64, :] + y_recv[64:128, :]
    lane64 = lanes((64, LANE))
    masked = jnp.concatenate([jnp.where(lane64 // 32 == q, d_all, 0.0) for q in range(4)], 0)
    v_all = dot(masked, cz[...])
    lane8 = lanes((8, LANE))
    signs = []
    for d in range(8):
        sign_z = jnp.where(lane8 % 64 >= 32, sign(d, 2), 1.0)
        signs.append(sign_z * jnp.where(lane8 >= 64, sign(d, 0), 1.0))
    v_all = v_all * jnp.concatenate(signs * 4, 0)
    o_all = dot(cx[...], v_all)
    lane_r = lanes((32, LANE))
    left = lane_r < 64
    r2 = jnp.where(left, o_all[0:32], o_all[32:64])
    for k in range(16):
        z_send[k] = r2[2 * k : 2 * k + 2]

    def z_copy(z, slot):
        return pltpu.make_async_remote_copy(
            src_ref=z_send.at[z], dst_ref=z_recv.at[slot], send_sem=zs.at[z],
            recv_sem=zr.at[slot], device_id=at_z(z), device_id_type=MESH,
        )

    def z_start(o, carry):
        z_copy(turn(zi + o, 16), zi).start()
        return carry

    def z_wait(o, carry):
        z_copy(turn(zi + o, 16), turn(zi - o + 16, 16)).wait_recv()
        return carry

    lax.fori_loop(1, 16, z_start, 0)
    z_recv[zi] = z_send[zi]
    lax.fori_loop(1, 16, z_wait, 0)
    total = z_recv[0]
    for k in range(1, 16):
        total = total + z_recv[k]
    z_all[zi] = total

    def a_copy(z, slot):
        return pltpu.make_async_remote_copy(
            src_ref=z_all.at[zi], dst_ref=z_all.at[slot], send_sem=as_.at[z],
            recv_sem=ar.at[slot], device_id=at_z(z), device_id_type=MESH,
        )

    def a_start(o, carry):
        a_copy(turn(zi + o, 16), zi).start()
        return carry

    def a_wait(o, carry):
        a_copy(turn(zi + o, 16), turn(zi - o + 16, 16)).wait_recv()
        return carry

    lax.fori_loop(1, 16, a_start, 0)
    lax.fori_loop(1, 16, a_wait, 0)
    for k in range(16):
        r2_ref[2 * k : 2 * k + 2, :] = z_all[k]

    r2 = r2_ref[...]
    lam = lam2[...] + lam_y[xi * 16 + yc]
    factor = jnp.where(lam == 0.0, 0.0, 4.0 * math.pi / jnp.where(lam == 0.0, 1.0, lam))
    phi2 = r2 * factor
    top = jnp.where(left, r2, roll(phi2, 64))
    bottom = jnp.where(left, roll(r2, 64), phi2)
    t_all = dot(xall[...], jnp.concatenate([top, bottom], 0))
    t0, t1, t2 = t_all[0:40], t_all[40:80], t_all[80:120]
    left40 = lanes((40, LANE)) < 64
    of_rho = jnp.concatenate([jnp.where(left40, t0, roll(t1, 64)), t2], 1)
    of_phi = jnp.concatenate([jnp.where(left40, roll(t0, 64), t1), roll(t2, 64)], 1)
    planes = dot(jnp.concatenate([of_rho, of_phi], 0), zt[...])
    for d in range(8):
        both = planes[:, 0:LANE] + sign(d, 2) * planes[:, LANE : 2 * LANE]
        for f in range(2):
            rows20 = both[40 * f : 40 * f + 20] + sign(d, 0) * both[40 * f + 20 : 40 * f + 40]
            for h in range(2):
                at = (2 * d + h) * PART + 10 * f
                c_send[at : at + 10, :] = rows20[10 * h : 10 * h + 10]

    def c_copy(c, slot):
        return pltpu.make_async_remote_copy(
            src_ref=c_send.at[rows(lax.rem(c, 8), 2 * PART)],
            dst_ref=c_recv.at[rows(slot, 2 * PART)], send_sem=cs.at[c],
            recv_sem=cr.at[slot], device_id=at_y(c), device_id_type=MESH,
        )

    def c_start(o, carry):
        c_copy(turn(yc + o, 16), yc).start()
        return carry

    lax.fori_loop(1, 16, c_start, 0)
    c_recv[rows(yc, 2 * PART), :] = c_send[rows(dom, 2 * PART), :]

    def f_copy(x, c, from_x):
        return pltpu.make_async_remote_copy(
            src_ref=c_recv.at[rows(2 * c + lax.rem(x, 2), PART)],
            dst_ref=f_recv.at[rows(from_x * 16 + c, PART)],
            send_sem=fs.at[x * 16 + c], recv_sem=fr.at[from_x * 16 + c],
            device_id=at_x(x), device_id_type=MESH,
        )

    def forward(c):
        for o in (2, 1, 3):
            f_copy(turn(xi + o, 4), c, xi).start()
        f_recv[rows(xi * 16 + c, PART), :] = c_recv[rows(2 * c + s, PART), :]

    forward(yc)

    def c_wait(o, carry):
        c = turn(yc - o + 16, 16)
        c_copy(turn(yc + o, 16), c).wait_recv()
        forward(c)
        return carry

    lax.fori_loop(1, 16, c_wait, 0)

    halo2.wait()
    lane40 = lanes((SIDE, LANE))
    for r in range(ROWS):
        own = jnp.where(lane40 < 2 * GAP, buf_a[r, 8:48, :], 0.0)
        if r < HALO:
            inside = (lane40 >= 2 * GAP) & (lane40 < 2 * GAP + SIDE)
            own = jnp.where(inside, roll(h2_recv[HALO - 1 - r], GAP), own)
        field[r] = own

    def f_wait(c, carry):
        for o in (1, 3, 2):
            f_copy(turn(xi + o, 4), c, turn(xi - o + 4, 4)).wait_recv()
        return carry

    lax.fori_loop(0, 16, f_wait, 0)

    odd_col = lanes((SIDE, GRID)) >= 32
    to_y = jnp.where(odd_col, sign_y, 1.0) * yt[...]
    for r in range(ROWS):
        rho = dot(to_y, f_recv[pl.ds(r, GRID, stride=PART), :])
        phi = dot(to_y, f_recv[pl.ds(ROWS + r, GRID, stride=PART), :])
        coef_out[r] = coef[r] + (phi + EXCHANGE * cbrt(rho)) * (2.0 / HALF_WIDTH)

    for o in range(1, 4):
        x_copy(turn(xi + o, 4), xi).wait_send()

    def finish(o, carry):
        y_copy(turn(yc + o, 16), yc).wait_send()
        z_copy(turn(zi + o, 16), zi).wait_send()
        a_copy(turn(zi + o, 16), zi).wait_send()
        c_copy(turn(yc + o, 16), yc).wait_send()
        return carry

    lax.fori_loop(1, 16, finish, 0)

    def f_finish(c, carry):
        for o in range(1, 4):
            f_copy(turn(xi + o, 4), c, xi).wait_send()
        return carry

    lax.fori_loop(0, 16, f_finish, 0)


def last_kernel(field, coef, out, buf_a, buf_b, lines):
    band = lax.axis_index("band")
    s = lax.rem(band, 2)
    clear_edges(buf_a)
    clear_edges(buf_b)
    for r in range(ROWS):
        buf_a[r, 8:48, :] = field[r]
    chebyshev(buf_a, buf_b, coef)
    for slot in range(20):
        g, r = divmod(slot, ROWS)
        row = slot + s * (19 - 2 * slot)
        lines[pl.ds(row, SIDE, stride=24), :] = roll(buf_a[r, 8:48, :], -GAP * g)
    lane = lanes((24, LANE))
    for block in range(13):
        acc = jnp.zeros((24, LANE), F32)
        for y in range(SIDE):
            start = SIDE * y - LANE * block
            if start + SIDE > 0 and start < LANE:
                v = roll(lines[y * 24 : y * 24 + 24, :], start)
                inside = (lane >= start) & (lane < start + SIDE)
                acc = jnp.where(inside, v, acc)
        width = min(LANE, 1600 - LANE * block)
        out[:, block * LANE : block * LANE + width] = acc[0:20, 0:width]


def local(psi_in, v_in, offsets):
    consts, lam = tables()
    vmem = pl.BlockSpec(memory_space=pltpu.VMEM)
    smem = pl.BlockSpec(memory_space=pltpu.SMEM)
    dma = pltpu.SemaphoreType.DMA
    tile = jax.ShapeDtypeStruct((ROWS, SIDE, LANE), F32)

    def scratch(*shape):
        return pltpu.VMEM(shape, F32)

    field, coef = pl.pallas_call(
        main_kernel,
        out_shape=(tile, tile),
        in_specs=[smem, smem] + [vmem] * 9,
        out_specs=(vmem, vmem),
        scratch_shapes=[
            scratch(24, 1664), scratch(40, 1664), scratch(40 * 32, LANE), scratch(40 * 40, LANE),
            scratch(8, 1664), scratch(8, 1664), scratch(ROWS, 56, LANE), scratch(ROWS, 56, LANE),
            scratch(ROWS, SIDE, LANE), scratch(32, 512),
            scratch(4, 16, 512), scratch(4, 16, 512), scratch(128, LANE), scratch(128, LANE),
            scratch(16, 2, LANE), scratch(16, 2, LANE), scratch(16, 2, LANE), scratch(32, LANE),
            scratch(16 * PART, LANE), scratch(32 * PART, LANE), scratch(64 * PART, LANE),
            scratch(HALO, SIDE, LANE),
            dma((2,)), dma((2,)), dma((4,)), dma((4,)), dma((16,)), dma((16,)), dma((16,)),
            dma((16,)), dma((16,)), dma((16,)), dma((16,)), dma((16,)), dma((64,)), dma((64,)),
        ],
        compiler_params=pltpu.CompilerParams(collective_id=0, has_side_effects=True),
        name="step",
    )(offsets, jnp.asarray(lam), psi_in[0, 0], v_in[0], *[jnp.asarray(a) for a in consts])
    out = pl.pallas_call(
        last_kernel,
        out_shape=jax.ShapeDtypeStruct((20, 1600), F32),
        in_specs=[vmem, vmem],
        out_specs=vmem,
        scratch_shapes=[
            scratch(ROWS, 56, LANE), scratch(ROWS, 56, LANE), scratch(40 * 24, LANE),
        ],
        name="last",
    )(field, coef)
    return out[None, None]


def solution(mesh):
    return jax.shard_map(
        local,
        mesh=mesh,
        in_specs=(P("dom", "band", None, None), P("dom", None, None), P()),
        out_specs=P("dom", "band", None, None),
        check_vma=False,
    )
```

time: 602 us -> 83.5 us (0.14)
  the two profiles are of different devices: /device:TPU:4 before, /device:TPU:1 now
where the time goes in v1:
time: 83.5 us; the launch traced here: 83.3 us
  Pallas kernels  78.6 us (94%)
  local copies, waits for them, and re-layouts  4.64 us (6%)
    pallas_call x1, Pallas kernels, local(): pl.pallas_call(main_kernel, out_shape=(tile, tile), in_specs=[smem, smem]...  75.1 us
    pallas_call x1, Pallas kernels, local(): pl.pallas_call(last_kernel, out_shape=jax.ShapeDtypeStruct((20, 1600), F3...  3.53 us
    unnamed x2, local copies, waits for them, and re-layouts  2.93 us
    broadcast_in_dim x1, local copies, waits for them, and re-layouts, local(): return out[None, None]  1.71 us

profile of v1, /device:TPU:1, one launch (start us, length us, event | category | flops | bytes accessed | tf_op | source)
XLA Modules:
  0.0 83.3 jit_solution(14153623842895794085)
XLA Ops:
  0.0 1.3 %copy.12.offs = s32[8,3]{1,0:T(8,128)} copy(s32[8,3]{0,1:T(4,128)} %param.13) | data formatting | bytes 192 | tf_op args[2]
  1.3 1.6 %copy.16 = f32[1,1,20,1600]{3,2,1,0:T(8,128)} copy(f32[1,1,20,1600]{3,1,2,0:T(1,128)} %param.11) | data formatting | bytes 256000
  2.9 75.1 %step.1 = (f32[10,40,128]{2,1,0:T(8,128)}, f32[10,40,128]{2,1,0:T(8,128)}) custom-call(s32[8,3]{1,0:T(8,128)} %copy.12.offs, f32[64]{0:T(128)} %constant.16.clone.lam_y, f32[20,1600]{1,0:T(8,128)} %bitcast.5, f32[40,1600]{1,0:T(8,128)} %bitcast.7, f32[32,128]{1,0:T(8,128)} %constant.17.clone.lam2, f32[64,32]{1,0:T(8,128)} %constant.18.clone.by, ...), custom_call_target="tpu_custom_call" | custom-call | tf_op jit(solution)/shard_map/step/pallas_call | solution.py:500
  78.0 3.5 %last.1 = f32[20,1600]{1,0:T(8,128)} custom-call(f32[10,40,128]{2,1,0:T(8,128)} %get-tuple-element.7.field, f32[10,40,128]{2,1,0:T(8,128)} %get-tuple-element.8.coef), custom_call_target="tpu_custom_call" | custom-call | tf_op jit(solution)/shard_map/last/pallas_call | solution.py:519
  81.6 1.7 %copy.13 = f32[1,1,20,1600]{3,1,2,0:T(1,128)} copy(f32[1,1,20,1600]{3,2,1,0:T(8,128)} %bitcast.6) | data formatting | bytes 256000 | tf_op jit(solution)/shard_map/broadcast_in_dim | solution.py:529

commit v2 on v1

--- a/solution.py
+++ b/solution.py
@@ -23,6 +23,10 @@
 HALF_WIDTH = 4.5
 EXCHANGE = -((3.0 / math.pi) ** (1.0 / 3.0))
 PART = 24
+USED = 20
+TABLES = 8
+NEAR = [o for m in range(1, 8) for o in (m, 16 - m)] + [8]
+FAR = NEAR[::-1]
 
 
 def wave_list():
@@ -75,8 +79,9 @@
     lam2 = np.concatenate(
         [lam[:32, None] + lam[None, :], lam[32:, None] + lam[None, :]], axis=1
     )
-    out = (lam2, by, cz, cx, xall, zt, yt)
-    return [np.asarray(a, np.float32) for a in out], np.asarray(lam, np.float32)
+    lam_y = np.repeat(lam[:, None], LANE, axis=1)
+    out = (lam2, lam_y, by, cz, cx, xall, zt, yt)
+    return [np.asarray(a, np.float32) for a in out]
 
 
 def lanes(shape):
@@ -175,12 +180,21 @@
 
 
 def main_kernel(
-    offs, lam_y, psi, pot, lam2, by, cz, cx, xall, zt, yt,
-    field, coef_out,
-    psi_pad, pot_pad, lines, pot_lines, h_send, h_recv, buf_a, buf_b, coef, squares,
+    offs_in, psi, pot, *rest
+):
+    sources, rest = rest[:TABLES], rest[TABLES:]
+    field, coef_out, *rest = rest
+    copies, rest = rest[:TABLES], rest[TABLES:]
+    lam2, lam_y, by, cz, cx, xall, zt, yt = copies
+    (
+    offs, psi_raw, pot_raw, in_sems, psi_pad, pot_pad, lines, pot_lines, h_send, h_recv, buf_a, buf_b, coef, squares,
     p_send, x_recv, y_send, y_recv, z_send, z_recv, z_all, r2_ref, c_send, c_recv, f_recv, h2_recv,
     h_sems, h2_sems, xs, xr, ys, yr, zs, zr, as_, ar, cs, cr, fs, fr,
-):
+    ) = rest
+    loads = [
+        pltpu.make_async_copy(a, b, in_sems.at[n])
+        for n, (a, b) in enumerate(zip((psi, pot, offs_in, *sources), (psi_raw, pot_raw, offs, *copies)))
+    ]
     dom, band, xi, zi, yh = place()
     yc = yh * 8 + dom
     s = lax.rem(xi, 2)
@@ -193,26 +207,30 @@
         return (dom, yh * 64 + z * 4 + xi)
 
     def at_y(c):
-        return (lax.rem(c, 8), (c // 8) * 64 + zi * 4 + xi)
+        high = jnp.where(c >= 8, 1, 0)
+        return (c - 8 * high, high * 64 + zi * 4 + xi)
 
     def turn(value, n):
-        return lax.rem(value + n, n)
+        return jnp.where(value >= n, value - n, value)
 
     barrier = pltpu.get_barrier_semaphore()
-    for o in range(1, 4):
+    for o in FAR:
+        to = at_z(turn(zi + o, 16))
+        pl.semaphore_signal(barrier, inc=1, device_id=to, device_id_type=MESH)
+    for o in FAR:
+        to = at_y(turn(yc + o, 16))
+        pl.semaphore_signal(barrier, inc=1, device_id=to, device_id_type=MESH)
+    for o in (2, 1, 3):
         pl.semaphore_signal(barrier, inc=1, device_id=at_x(turn(xi + o, 4)), device_id_type=MESH)
-
-    def greet(o, carry):
-        pl.semaphore_signal(barrier, inc=1, device_id=at_z(turn(zi + o, 16)), device_id_type=MESH)
-        pl.semaphore_signal(barrier, inc=1, device_id=at_y(turn(yc + o, 16)), device_id_type=MESH)
-        return carry
-
-    lax.fori_loop(1, 16, greet, 0)
+    for load in loads:
+        load.start()
 
     upper = s.astype(F32)
-    h_send[:, 0:1600] = psi[12:20, :] * (1.0 - upper) + psi[0:8, :] * upper
-    psi_pad[0:20, 0:1600] = psi[...]
-    pot_pad[:, 0:1600] = pot[...]
+    loads[0].wait()
+    psi_pad[0:20, 0:1600] = psi_raw[...].reshape(20, 1600)
+    h_send[...] = psi_pad[12:20, :] * (1.0 - upper) + psi_pad[0:8, :] * upper
+    loads[1].wait()
+    pot_pad[:, 0:1600] = pot_raw[...]
     for y in range(SIDE):
         lines[y * 32 + 8 : y * 32 + 32, :] = line_of(psi_pad, 24, y)
     for y in range(SIDE):
@@ -224,6 +242,8 @@
             pot_lines, 40, lambda slot: slot + s * (39 - 2 * slot), r
         ) * (2.0 / HALF_WIDTH)
 
+    for load in loads[2:]:
+        load.wait()
     pl.semaphore_wait(barrier, 33)
 
     halo = pltpu.make_async_remote_copy(
@@ -253,10 +273,13 @@
             acc = jnp.where(lane32 // 32 == q, v, acc)
         squares[:, t * LANE : (t + 1) * LANE] = acc * acc * (1.0 / 64.0)
 
+    corners = 1.0 - offs[...].astype(F32) * (1.0 / 16.0)
+
     def sign(d, axis):
-        return 1.0 - offs[d, axis].astype(F32) * (1.0 / 16.0)
-
-    sign_y = sign(dom, 1)
+        return corners[axis : axis + 1, d : d + 1]
+
+    own_dom = lax.broadcasted_iota(jnp.int32, (1, 8), 1) == dom
+    sign_y = jnp.sum(jnp.where(own_dom, corners[1:2], 0.0), axis=1, keepdims=True)
     odd_row = lax.broadcasted_iota(jnp.int32, (GRID, 32), 0) >= 32
     parts = dot(jnp.where(odd_row, sign_y, 1.0) * by[...], squares[...])
     for x in range(4):
@@ -288,21 +311,25 @@
 
     def y_copy(c, slot):
         return pltpu.make_async_remote_copy(
-            src_ref=y_send.at[rows(c, 8)], dst_ref=y_recv.at[rows(slot, 8)], send_sem=ys.at[c],
-            recv_sem=yr.at[slot], device_id=at_y(c), device_id_type=MESH,
-        )
-
-    def y_start(o, carry):
+            src_ref=y_send.at[rows(c, 8)], dst_ref=y_recv.at[rows(slot, 8)], send_sem=ys,
+            recv_sem=yr, device_id=at_y(c), device_id_type=MESH,
+        )
+
+    def whole(ref, send_sem, recv_sem):
+        return pltpu.make_async_remote_copy(
+            src_ref=ref, dst_ref=ref, send_sem=send_sem, recv_sem=recv_sem,
+            device_id=at_x(partner), device_id_type=MESH,
+        )
+
+    y_whole = whole(y_recv.at[0:120], ys, yr)
+    z_whole = whole(z_recv.at[0:15], zs, zr)
+    a_whole = whole(z_all.at[0:15], as_, ar)
+    f_whole = whole(f_recv.at[0 : 48 * USED], fs, fr)
+
+    for o in FAR:
         y_copy(turn(yc + o, 16), yc).start()
-        return carry
-
-    def y_wait(o, carry):
-        y_copy(turn(yc + o, 16), turn(yc - o + 16, 16)).wait_recv()
-        return carry
-
-    lax.fori_loop(1, 16, y_start, 0)
     y_recv[rows(yc, 8), :] = y_send[rows(yc, 8), :]
-    lax.fori_loop(1, 16, y_wait, 0)
+    y_whole.wait_recv()
 
     d_all = y_recv[0:64, :] + y_recv[64:128, :]
     lane64 = lanes((64, LANE))
@@ -323,21 +350,14 @@
 
     def z_copy(z, slot):
         return pltpu.make_async_remote_copy(
-            src_ref=z_send.at[z], dst_ref=z_recv.at[slot], send_sem=zs.at[z],
-            recv_sem=zr.at[slot], device_id=at_z(z), device_id_type=MESH,
-        )
-
-    def z_start(o, carry):
+            src_ref=z_send.at[z], dst_ref=z_recv.at[slot], send_sem=zs,
+            recv_sem=zr, device_id=at_z(z), device_id_type=MESH,
+        )
+
+    for o in FAR:
         z_copy(turn(zi + o, 16), zi).start()
-        return carry
-
-    def z_wait(o, carry):
-        z_copy(turn(zi + o, 16), turn(zi - o + 16, 16)).wait_recv()
-        return carry
-
-    lax.fori_loop(1, 16, z_start, 0)
     z_recv[zi] = z_send[zi]
-    lax.fori_loop(1, 16, z_wait, 0)
+    z_whole.wait_recv()
     total = z_recv[0]
     for k in range(1, 16):
         total = total + z_recv[k]
@@ -345,25 +365,18 @@
 
     def a_copy(z, slot):
         return pltpu.make_async_remote_copy(
-            src_ref=z_all.at[zi], dst_ref=z_all.at[slot], send_sem=as_.at[z],
-            recv_sem=ar.at[slot], device_id=at_z(z), device_id_type=MESH,
-        )
-
-    def a_start(o, carry):
+            src_ref=z_all.at[zi], dst_ref=z_all.at[slot], send_sem=as_,
+            recv_sem=ar, device_id=at_z(z), device_id_type=MESH,
+        )
+
+    for o in FAR:
         a_copy(turn(zi + o, 16), zi).start()
-        return carry
-
-    def a_wait(o, carry):
-        a_copy(turn(zi + o, 16), turn(zi - o + 16, 16)).wait_recv()
-        return carry
-
-    lax.fori_loop(1, 16, a_start, 0)
-    lax.fori_loop(1, 16, a_wait, 0)
+    a_whole.wait_recv()
     for k in range(16):
         r2_ref[2 * k : 2 * k + 2, :] = z_all[k]
 
     r2 = r2_ref[...]
-    lam = lam2[...] + lam_y[xi * 16 + yc]
+    lam = lam2[...] + lam_y[pl.ds(xi * 16 + yc, 1), :]
     factor = jnp.where(lam == 0.0, 0.0, 4.0 * math.pi / jnp.where(lam == 0.0, 1.0, lam))
     phi2 = r2 * factor
     top = jnp.where(left, r2, roll(phi2, 64))
@@ -382,42 +395,46 @@
                 at = (2 * d + h) * PART + 10 * f
                 c_send[at : at + 10, :] = rows20[10 * h : 10 * h + 10]
 
-    def c_copy(c, slot):
-        return pltpu.make_async_remote_copy(
-            src_ref=c_send.at[rows(lax.rem(c, 8), 2 * PART)],
-            dst_ref=c_recv.at[rows(slot, 2 * PART)], send_sem=cs.at[c],
+    def used(index):
+        return pl.ds(pl.multiple_of(index * PART, 8), USED)
+
+    def c_copy(c, slot, h):
+        return pltpu.make_async_remote_copy(
+            src_ref=c_send.at[used(2 * (c - jnp.where(c >= 8, 8, 0)) + h)],
+            dst_ref=c_recv.at[used(2 * slot + h)], send_sem=cs,
             recv_sem=cr.at[slot], device_id=at_y(c), device_id_type=MESH,
         )
 
-    def c_start(o, carry):
-        c_copy(turn(yc + o, 16), yc).start()
-        return carry
-
-    lax.fori_loop(1, 16, c_start, 0)
+    for o in NEAR:
+        for h in range(2):
+            c_copy(turn(yc + o, 16), yc, h).start()
     c_recv[rows(yc, 2 * PART), :] = c_send[rows(dom, 2 * PART), :]
 
-    def f_copy(x, c, from_x):
-        return pltpu.make_async_remote_copy(
-            src_ref=c_recv.at[rows(2 * c + lax.rem(x, 2), PART)],
-            dst_ref=f_recv.at[rows(from_x * 16 + c, PART)],
-            send_sem=fs.at[x * 16 + c], recv_sem=fr.at[from_x * 16 + c],
+    def f_copy(x, h, c, from_x):
+        return pltpu.make_async_remote_copy(
+            src_ref=c_recv.at[used(2 * c + h)],
+            dst_ref=f_recv.at[used(from_x * 16 + c)],
+            send_sem=fs, recv_sem=fr,
             device_id=at_x(x), device_id_type=MESH,
         )
 
     def forward(c):
         for o in (2, 1, 3):
-            f_copy(turn(xi + o, 4), c, xi).start()
+            f_copy(turn(xi + o, 4), s if o == 2 else 1 - s, c, xi).start()
         f_recv[rows(xi * 16 + c, PART), :] = c_recv[rows(2 * c + s, PART), :]
 
     forward(yc)
 
-    def c_wait(o, carry):
+    y_whole.wait_send()
+    z_whole.wait_send()
+    a_whole.wait_send()
+    for o in range(1, 4):
+        x_copy(turn(xi + o, 4), xi).wait_send()
+
+    for o in NEAR:
         c = turn(yc - o + 16, 16)
-        c_copy(turn(yc + o, 16), c).wait_recv()
+        whole(c_recv.at[0 : 2 * USED], cs, cr.at[c]).wait_recv()
         forward(c)
-        return carry
-
-    lax.fori_loop(1, 16, c_wait, 0)
 
     halo2.wait()
     lane40 = lanes((SIDE, LANE))
@@ -428,12 +445,7 @@
             own = jnp.where(inside, roll(h2_recv[HALO - 1 - r], GAP), own)
         field[r] = own
 
-    def f_wait(c, carry):
-        for o in (1, 3, 2):
-            f_copy(turn(xi + o, 4), c, turn(xi - o + 4, 4)).wait_recv()
-        return carry
-
-    lax.fori_loop(0, 16, f_wait, 0)
+    f_whole.wait_recv()
 
     odd_col = lanes((SIDE, GRID)) >= 32
     to_y = jnp.where(odd_col, sign_y, 1.0) * yt[...]
@@ -441,25 +453,8 @@
         rho = dot(to_y, f_recv[pl.ds(r, GRID, stride=PART), :])
         phi = dot(to_y, f_recv[pl.ds(ROWS + r, GRID, stride=PART), :])
         coef_out[r] = coef[r] + (phi + EXCHANGE * cbrt(rho)) * (2.0 / HALF_WIDTH)
-
-    for o in range(1, 4):
-        x_copy(turn(xi + o, 4), xi).wait_send()
-
-    def finish(o, carry):
-        y_copy(turn(yc + o, 16), yc).wait_send()
-        z_copy(turn(zi + o, 16), zi).wait_send()
-        a_copy(turn(zi + o, 16), zi).wait_send()
-        c_copy(turn(yc + o, 16), yc).wait_send()
-        return carry
-
-    lax.fori_loop(1, 16, finish, 0)
-
-    def f_finish(c, carry):
-        for o in range(1, 4):
-            f_copy(turn(xi + o, 4), c, xi).wait_send()
-        return carry
-
-    lax.fori_loop(0, 16, f_finish, 0)
+    whole(c_recv.at[0 : 30 * USED], cs, cs).wait_send()
+    f_whole.wait_send()
 
 
 def last_kernel(field, coef, out, buf_a, buf_b, lines):
@@ -484,25 +479,30 @@
                 inside = (lane >= start) & (lane < start + SIDE)
                 acc = jnp.where(inside, v, acc)
         width = min(LANE, 1600 - LANE * block)
-        out[:, block * LANE : block * LANE + width] = acc[0:20, 0:width]
+        for x in range(20):
+            out[x, :, block * LANE : block * LANE + width] = acc[x : x + 1, 0:width]
 
 
 def local(psi_in, v_in, offsets):
-    consts, lam = tables()
+    consts = tables()
     vmem = pl.BlockSpec(memory_space=pltpu.VMEM)
-    smem = pl.BlockSpec(memory_space=pltpu.SMEM)
     dma = pltpu.SemaphoreType.DMA
     tile = jax.ShapeDtypeStruct((ROWS, SIDE, LANE), F32)
 
     def scratch(*shape):
         return pltpu.VMEM(shape, F32)
 
+    operands = (
+        offsets.T, jnp.swapaxes(psi_in[0], 0, 1), v_in[0], *[jnp.asarray(a) for a in consts]
+    )
     field, coef = pl.pallas_call(
         main_kernel,
         out_shape=(tile, tile),
-        in_specs=[smem, smem] + [vmem] * 9,
+        in_specs=[pl.BlockSpec(memory_space=pltpu.HBM)] * (3 + TABLES),
         out_specs=(vmem, vmem),
         scratch_shapes=[
+            *[scratch(*a.shape) for a in consts], pltpu.VMEM((3, 8), jnp.int32),
+            scratch(20, 1, 1600), scratch(40, 1600), dma((3 + TABLES,)),
             scratch(24, 1664), scratch(40, 1664), scratch(40 * 32, LANE), scratch(40 * 40, LANE),
             scratch(8, 1664), scratch(8, 1664), scratch(ROWS, 56, LANE), scratch(ROWS, 56, LANE),
             scratch(ROWS, SIDE, LANE), scratch(32, 512),
@@ -510,23 +510,25 @@
             scratch(16, 2, LANE), scratch(16, 2, LANE), scratch(16, 2, LANE), scratch(32, LANE),
             scratch(16 * PART, LANE), scratch(32 * PART, LANE), scratch(64 * PART, LANE),
             scratch(HALO, SIDE, LANE),
-            dma((2,)), dma((2,)), dma((4,)), dma((4,)), dma((16,)), dma((16,)), dma((16,)),
-            dma((16,)), dma((16,)), dma((16,)), dma((16,)), dma((16,)), dma((64,)), dma((64,)),
+            dma((2,)), dma((2,)), dma((4,)), dma((4,)), dma, dma, dma, dma, dma, dma,
+            dma, dma((16,)), dma, dma,
         ],
-        compiler_params=pltpu.CompilerParams(collective_id=0, has_side_effects=True),
+        compiler_params=pltpu.CompilerParams(collective_id=0, has_side_effects=True, vmem_limit_bytes=24 << 20
+        ),
         name="step",
-    )(offsets, jnp.asarray(lam), psi_in[0, 0], v_in[0], *[jnp.asarray(a) for a in consts])
+    )(*[pltpu.with_memory_space_constraint(a, pltpu.HBM) for a in operands])
     out = pl.pallas_call(
         last_kernel,
-        out_shape=jax.ShapeDtypeStruct((20, 1600), F32),
+        out_shape=jax.ShapeDtypeStruct((20, 1, 1600), F32),
         in_specs=[vmem, vmem],
         out_specs=vmem,
         scratch_shapes=[
             scratch(ROWS, 56, LANE), scratch(ROWS, 56, LANE), scratch(40 * 24, LANE),
         ],
+        compiler_params=pltpu.CompilerParams(vmem_limit_bytes=8 << 20),
         name="last",
     )(field, coef)
-    return out[None, None]
+    return jnp.swapaxes(out, 0, 1)[None]
 
 
 def solution(mesh):

time: 83.5 us -> 68.3 us (0.82)
  Pallas kernels: 78.6 us -> 68.1 us
  local copies, waits for them, and re-layouts: 4.64 us -> 0 us
    pallas_call x2, Pallas kernels: 78.6 us -> 68.1 us  [the longest x1 65.5 us: local(): pl.pallas_call(main_kernel, out_shape=(tile, tile), in_specs=[pl.BlockSpe...]
    unnamed x2 -> x0, local copies, waits for them, and re-layouts: 2.93 us -> none
    broadcast_in_dim x1 -> x0, local copies, waits for them, and re-layouts: 1.71 us -> none  [local(): return out[None, None]]
where the time goes in v2:
time: 68.3 us; the launch traced here: 68.1 us
  Pallas kernels  68.1 us (100%)
    pallas_call x1, Pallas kernels, local(): pl.pallas_call(main_kernel, out_shape=(tile, tile), in_specs=[pl.BlockSpe...  65.5 us
    pallas_call x1, Pallas kernels, local(): pl.pallas_call(last_kernel, out_shape=jax.ShapeDtypeStruct((20, 1, 1600),...  2.61 us

profile of v2, /device:TPU:1, one launch (start us, length us, event | category | flops | bytes accessed | tf_op | source)
XLA Modules:
  0.0 68.1 jit_solution(10766545950979841675)
XLA Ops:
  0.0 65.5 %step.1 = (f32[10,40,128]{2,1,0:T(8,128)S(1)}, f32[10,40,128]{2,1,0:T(8,128)S(1)}) custom-call(s32[3,8]{1,0:T(4,128)} %bitcast.8, f32[20,1,1600]{2,1,0:T(1,128)} %bitcast.7, f32[40,1600]{1,0:T(8,128)} %bitcast.6, f32[32,128]{1,0:T(8,128)} %constant.16.clone.rest_0_, f32[64,128]{1,0:T(8,128)} %constant.17.clone.rest_1_, f32[64,32]{1,0:T(8,128)} %constant.18.clone.rest_2_, ...), custom_call_target="tpu_custom_call" | custom-call | tf_op jit(solution)/shard_map/step/pallas_call | solution.py:498
  65.5 2.6 %last.1 = f32[20,1,1600]{2,1,0:T(1,128)} custom-call(f32[10,40,128]{2,1,0:T(8,128)S(1)} %get-tuple-element.7.field, f32[10,40,128]{2,1,0:T(8,128)S(1)} %get-tuple-element.8.coef), custom_call_target="tpu_custom_call" | custom-call | tf_op jit(solution)/shard_map/last/pallas_call | solution.py:520

commit v3 on v2

--- a/solution.py
+++ b/solution.py
@@ -27,6 +27,8 @@
 TABLES = 8
 NEAR = [o for m in range(1, 8) for o in (m, 16 - m)] + [8]
 FAR = NEAR[::-1]
+FIRST_SUM = 12
+SUM_TO = (0, 1, 2, 3, 4, 11, 5, 10, 6, 9, 7, 8, 12, 13, 14, 15)
 
 
 def wave_list():
@@ -116,10 +118,11 @@
     return v
 
 
-def to_tiles(ref, stride, row_of, tile):
+def to_tiles(ref, stride, row_of, tile, groups=(0, 1, 2), acc=None):
     lane = lanes((SIDE, LANE))
-    acc = jnp.zeros((SIDE, LANE), F32)
-    for g in range(3):
+    if acc is None:
+        acc = jnp.zeros((SIDE, LANE), F32)
+    for g in groups:
         slot = ROWS * g + tile
         if slot < SLOTS:
             v = roll(ref[pl.ds(row_of(slot), SIDE, stride=stride), :], GAP * g)
@@ -187,9 +190,9 @@
     copies, rest = rest[:TABLES], rest[TABLES:]
     lam2, lam_y, by, cz, cx, xall, zt, yt = copies
     (
-    offs, psi_raw, pot_raw, in_sems, psi_pad, pot_pad, lines, pot_lines, h_send, h_recv, buf_a, buf_b, coef, squares,
-    p_send, x_recv, y_send, y_recv, z_send, z_recv, z_all, r2_ref, c_send, c_recv, f_recv, h2_recv,
-    h_sems, h2_sems, xs, xr, ys, yr, zs, zr, as_, ar, cs, cr, fs, fr,
+    offs, psi_raw, pot_raw, in_sems, psi_pad, pot_pad, lines, pot_lines, h_pad, h_recv, buf_a, buf_b, coef, squares,
+    p_send, x_recv, y_send, y_recv, z_send, z_recv, z_all, c_send, c_recv, f_recv, h2_recv,
+    ready2, ready3, h_sems, h2_sems, xs, xr, ys, yr, zs, zr, as_, ar, cs, cr, fs, fr,
     ) = rest
     loads = [
         pltpu.make_async_copy(a, b, in_sems.at[n])
@@ -214,54 +217,72 @@
         return jnp.where(value >= n, value - n, value)
 
     barrier = pltpu.get_barrier_semaphore()
-    for o in FAR:
-        to = at_z(turn(zi + o, 16))
-        pl.semaphore_signal(barrier, inc=1, device_id=to, device_id_type=MESH)
-    for o in FAR:
-        to = at_y(turn(yc + o, 16))
-        pl.semaphore_signal(barrier, inc=1, device_id=to, device_id_type=MESH)
+    def signal(sem, to):
+        pl.semaphore_signal(sem, inc=1, device_id=to, device_id_type=MESH)
+
+    core = lax.rem(dom, 2)
+    other = 1 - 2 * core
+
+    def at_y_near(lines, flip):
+        return at_y(turn(turn(yc + 2 * lines + 16, 16), 16) + flip * other)
+
+    for o in (2, 14, 1, 15):
+        signal(barrier, at_z(turn(zi + o, 16)))
     for o in (2, 1, 3):
-        pl.semaphore_signal(barrier, inc=1, device_id=at_x(turn(xi + o, 4)), device_id_type=MESH)
+        signal(barrier, at_x(turn(xi + o, 4)))
+    for n in (-1, 1):
+        signal(barrier, at_y_near(n, 0))
+        signal(barrier, at_y_near(n, 1))
+    signal(barrier, at_y_near(0, 1))
     for load in loads:
         load.start()
-
-    upper = s.astype(F32)
-    loads[0].wait()
-    psi_pad[0:20, 0:1600] = psi_raw[...].reshape(20, 1600)
-    h_send[...] = psi_pad[12:20, :] * (1.0 - upper) + psi_pad[0:8, :] * upper
-    loads[1].wait()
-    pot_pad[:, 0:1600] = pot_raw[...]
-    for y in range(SIDE):
-        lines[y * 32 + 8 : y * 32 + 32, :] = line_of(psi_pad, 24, y)
-    for y in range(SIDE):
-        pot_lines[y * 40 : y * 40 + 40, :] = line_of(pot_pad, 40, y)
-    clear_edges(buf_a)
-    clear_edges(buf_b)
-    for r in range(ROWS):
-        coef[r] = to_tiles(
-            pot_lines, 40, lambda slot: slot + s * (39 - 2 * slot), r
-        ) * (2.0 / HALF_WIDTH)
-
-    for load in loads[2:]:
-        load.wait()
-    pl.semaphore_wait(barrier, 33)
+    pl.semaphore_wait(barrier, 12)
 
     halo = pltpu.make_async_remote_copy(
-        src_ref=h_send, dst_ref=h_recv, send_sem=h_sems.at[0], recv_sem=h_sems.at[1],
+        src_ref=psi.at[pl.ds(12 - 12 * s, HALO)], dst_ref=h_recv, send_sem=h_sems.at[0], recv_sem=h_sems.at[1],
         device_id=at_x(partner), device_id_type=MESH,
     )
     halo.start()
-    halo.wait()
-    for y in range(SIDE):
-        lines[y * 32 : y * 32 + 8, :] = line_of(h_recv, 8, y)
+    for o in (2, 14):
+        signal(ready2, at_z(turn(zi + o, 16)))
+    for n in (-1, 1):
+        signal(ready2, at_y_near(n, 0))
+
+    clear_edges(buf_a)
+    clear_edges(buf_b)
+    loads[0].wait()
+    psi_pad[0:20, 0:1600] = psi_raw[...].reshape(20, 1600)
 
     def row_of(slot):
         if slot < 20:
             return 8 + slot + s * (19 - 2 * slot)
         return (slot - 20) + s * (47 - 2 * slot)
 
-    for r in range(ROWS):
-        buf_a[r, 8:48, :] = to_tiles(lines, 32, row_of, r)
+    for y in range(SIDE):
+        lines[y * 32 + 8 : y * 32 + 32, :] = line_of(psi_pad, 24, y)
+    for r in range(ROWS):
+        buf_a[r, 8:48, :] = to_tiles(lines, 32, row_of, r, (0, 1))
+    loads[1].wait()
+    pot_pad[:, 0:1600] = pot_raw[...]
+    for y in range(SIDE):
+        pot_lines[y * 40 : y * 40 + 40, :] = line_of(pot_pad, 40, y)
+    for r in range(ROWS):
+        coef[r] = to_tiles(
+            pot_lines, 40, lambda slot: slot + s * (39 - 2 * slot), r
+        ) * (2.0 / HALF_WIDTH)
+    for load in loads[2:]:
+        load.wait()
+    pl.semaphore_wait(ready2, 4)
+    for o in (4, 12):
+        signal(ready3, at_z(turn(zi + o, 16)))
+    for n in (-2, 2):
+        signal(ready3, at_y_near(n, 0))
+    halo.wait()
+    h_pad[:, 0:1600] = h_recv[...].reshape(HALO, 1600)
+    for y in range(SIDE):
+        lines[y * 32 : y * 32 + 8, :] = line_of(h_pad, 8, y)
+    for r in range(HALO):
+        buf_a[r, 8:48, :] = to_tiles(lines, 32, row_of, r, (2,), buf_a[r, 8:48, :])
     chebyshev(buf_a, buf_b, coef)
 
     lane32 = lanes((32, LANE))
@@ -322,10 +343,9 @@
         )
 
     y_whole = whole(y_recv.at[0:120], ys, yr)
-    z_whole = whole(z_recv.at[0:15], zs, zr)
-    a_whole = whole(z_all.at[0:15], as_, ar)
     f_whole = whole(f_recv.at[0 : 48 * USED], fs, fr)
 
+    pl.semaphore_wait(ready3, 4)
     for o in FAR:
         y_copy(turn(yc + o, 16), yc).start()
     y_recv[rows(yc, 8), :] = y_send[rows(yc, 8), :]
@@ -345,37 +365,47 @@
     lane_r = lanes((32, LANE))
     left = lane_r < 64
     r2 = jnp.where(left, o_all[0:32], o_all[32:64])
-    for k in range(16):
-        z_send[k] = r2[2 * k : 2 * k + 2]
-
-    def z_copy(z, slot):
+    z_send[...] = r2
+
+    tile_of = zi - FIRST_SUM
+    sums = zi >= FIRST_SUM
+
+    def z_copy(t, slot):
         return pltpu.make_async_remote_copy(
-            src_ref=z_send.at[z], dst_ref=z_recv.at[slot], send_sem=zs,
-            recv_sem=zr, device_id=at_z(z), device_id_type=MESH,
+            src_ref=z_send.at[8 * t : 8 * t + 8], dst_ref=z_recv.at[rows(slot, 8)], send_sem=zs,
+            recv_sem=zr, device_id=at_z(FIRST_SUM + t), device_id_type=MESH,
         )
 
-    for o in FAR:
-        z_copy(turn(zi + o, 16), zi).start()
-    z_recv[zi] = z_send[zi]
-    z_whole.wait_recv()
-    total = z_recv[0]
-    for k in range(1, 16):
-        total = total + z_recv[k]
-    z_all[zi] = total
-
-    def a_copy(z, slot):
-        return pltpu.make_async_remote_copy(
-            src_ref=z_all.at[zi], dst_ref=z_all.at[slot], send_sem=as_,
-            recv_sem=ar, device_id=at_z(z), device_id_type=MESH,
-        )
-
-    for o in FAR:
-        a_copy(turn(zi + o, 16), zi).start()
-    a_whole.wait_recv()
-    for k in range(16):
-        r2_ref[2 * k : 2 * k + 2, :] = z_all[k]
-
-    r2 = r2_ref[...]
+    for t in range(4):
+
+        @pl.when(zi != FIRST_SUM + t)
+        def _():
+            z_copy(t, zi).start()
+
+    @pl.when(sums)
+    def _():
+        z_recv[rows(zi, 8), :] = z_send[rows(tile_of, 8), :]
+        whole(z_recv.at[0:120], zs, zr).wait_recv()
+        total = z_recv[0:8]
+        for k in range(1, 16):
+            total = total + z_recv[8 * k : 8 * k + 8]
+        z_all[rows(tile_of, 8), :] = total
+        for z in SUM_TO:
+
+            @pl.when(zi != z)
+            def _():
+                pltpu.make_async_remote_copy(
+                    src_ref=z_all.at[rows(tile_of, 8)], dst_ref=z_all.at[rows(tile_of, 8)],
+                    send_sem=as_, recv_sem=ar, device_id=at_z(z), device_id_type=MESH,
+                ).start()
+
+        whole(z_all.at[0:24], as_, ar).wait_recv()
+
+    @pl.when(zi < FIRST_SUM)
+    def _():
+        whole(z_all.at[0:32], as_, ar).wait_recv()
+
+    r2 = z_all[...]
     lam = lam2[...] + lam_y[pl.ds(xi * 16 + yc, 1), :]
     factor = jnp.where(lam == 0.0, 0.0, 4.0 * math.pi / jnp.where(lam == 0.0, 1.0, lam))
     phi2 = r2 * factor
@@ -426,8 +456,16 @@
     forward(yc)
 
     y_whole.wait_send()
-    z_whole.wait_send()
-    a_whole.wait_send()
+
+    @pl.when(sums)
+    def _():
+        whole(z_send.at[0:24], zs, zr).wait_send()
+        whole(z_recv.at[0:120], as_, ar).wait_send()
+
+    @pl.when(zi < FIRST_SUM)
+    def _():
+        whole(z_send.at[0:32], zs, zr).wait_send()
+
     for o in range(1, 4):
         x_copy(turn(xi + o, 4), xi).wait_send()
 
@@ -504,12 +542,13 @@
             *[scratch(*a.shape) for a in consts], pltpu.VMEM((3, 8), jnp.int32),
             scratch(20, 1, 1600), scratch(40, 1600), dma((3 + TABLES,)),
             scratch(24, 1664), scratch(40, 1664), scratch(40 * 32, LANE), scratch(40 * 40, LANE),
-            scratch(8, 1664), scratch(8, 1664), scratch(ROWS, 56, LANE), scratch(ROWS, 56, LANE),
+            scratch(8, 1664), scratch(HALO, 1, 1600), scratch(ROWS, 56, LANE), scratch(ROWS, 56, LANE),
             scratch(ROWS, SIDE, LANE), scratch(32, 512),
             scratch(4, 16, 512), scratch(4, 16, 512), scratch(128, LANE), scratch(128, LANE),
-            scratch(16, 2, LANE), scratch(16, 2, LANE), scratch(16, 2, LANE), scratch(32, LANE),
+            scratch(32, LANE), scratch(128, LANE), scratch(32, LANE),
             scratch(16 * PART, LANE), scratch(32 * PART, LANE), scratch(64 * PART, LANE),
             scratch(HALO, SIDE, LANE),
+            pltpu.SemaphoreType.REGULAR, pltpu.SemaphoreType.REGULAR,
             dma((2,)), dma((2,)), dma((4,)), dma((4,)), dma, dma, dma, dma, dma, dma,
             dma, dma((16,)), dma, dma,
         ],

time: 68.3 us -> 62.9 us (0.921)
  Pallas kernels: 68.1 us -> 62.7 us
    pallas_call x1, Pallas kernels: 65.5 us -> 60.1 us  [local(): pl.pallas_call(main_kernel, out_shape=(tile, tile), in_specs=[pl.BlockSpe...]
where the time goes in v3:
time: 62.9 us; the launch traced here: 62.7 us
  Pallas kernels  62.7 us (100%)
    pallas_call x1, Pallas kernels, local(): pl.pallas_call(main_kernel, out_shape=(tile, tile), in_specs=[pl.BlockSpe...  60.1 us
    pallas_call x1, Pallas kernels, local(): pl.pallas_call(last_kernel, out_shape=jax.ShapeDtypeStruct((20, 1, 1600),...  2.61 us

profile of v3, /device:TPU:1, one launch (start us, length us, event | category | flops | bytes accessed | tf_op | source)
XLA Modules:
  0.0 62.7 jit_solution(5455869441935778580)
XLA Ops:
  0.0 60.1 %step.1 = (f32[10,40,128]{2,1,0:T(8,128)S(1)}, f32[10,40,128]{2,1,0:T(8,128)S(1)}) custom-call(s32[3,8]{1,0:T(4,128)} %bitcast.8, f32[20,1,1600]{2,1,0:T(1,128)} %bitcast.7, f32[40,1600]{1,0:T(8,128)} %bitcast.6, f32[32,128]{1,0:T(8,128)} %constant.16.clone.rest_0_, f32[64,128]{1,0:T(8,128)} %constant.17.clone.rest_1_, f32[64,32]{1,0:T(8,128)} %constant.18.clone.rest_2_, ...), custom_call_target="tpu_custom_call" | custom-call | tf_op jit(solution)/shard_map/step/pallas_call | solution.py:536
  60.1 2.6 %last.1 = f32[20,1,1600]{2,1,0:T(1,128)} custom-call(f32[10,40,128]{2,1,0:T(8,128)S(1)} %get-tuple-element.7.field, f32[10,40,128]{2,1,0:T(8,128)S(1)} %get-tuple-element.8.coef), custom_call_target="tpu_custom_call" | custom-call | tf_op jit(solution)/shard_map/last/pallas_call | solution.py:559

commit v4 on v3

--- a/solution.py
+++ b/solution.py
@@ -131,12 +131,13 @@
     return acc
 
 
-def filter_step(src, dst, coef, first):
+def filter_step(src, dst, coef, number):
+    first = number == 0
     lane = lanes((SIDE, LANE))
     inside = (lane < 3 * GAP) & (lane % GAP < SIDE)
     scale = (0.5 if first else 1.0) / HALF_WIDTH
     beta = jnp.where(inside, scale, 0.0).astype(F32)
-    for r in range(ROWS):
+    for r in [(number + n) % ROWS for n in range(ROWS)]:
         c = src[r, 8:48, :]
         if r == 0:
             below = jnp.where(lane >= GAP, roll(src[ROWS - 1, 8:48, :], GAP), 0.0)
@@ -155,15 +156,9 @@
 
 
 def chebyshev(buf_a, buf_b, coef):
-    filter_step(buf_a, buf_b, coef, True)
-    filter_step(buf_b, buf_a, coef, False)
-
-    def two(_, carry):
-        filter_step(buf_a, buf_b, coef, False)
-        filter_step(buf_b, buf_a, coef, False)
-        return carry
-
-    lax.fori_loop(0, (DEG - 2) // 2, two, 0)
+    for number in range(DEG):
+        src, dst = (buf_a, buf_b) if number % 2 == 0 else (buf_b, buf_a)
+        filter_step(src, dst, coef, number)
 
 
 def clear_edges(buf):

time: 62.9 us -> 61.9 us (0.984)
  Pallas kernels: 62.7 us -> 61.7 us
where the time goes in v4:
time: 61.9 us; the launch traced here: 61.7 us
  Pallas kernels  61.7 us (100%)
    pallas_call x1, Pallas kernels, local(): pl.pallas_call(main_kernel, out_shape=(tile, tile), in_specs=[pl.BlockSpe...  59.6 us
    pallas_call x1, Pallas kernels, local(): pl.pallas_call(last_kernel, out_shape=jax.ShapeDtypeStruct((20, 1, 1600),...  2.07 us

profile of v4, /device:TPU:1, one launch (start us, length us, event | category | flops | bytes accessed | tf_op | source)
XLA Modules:
  0.0 61.7 jit_solution(16916249038742096925)
XLA Ops:
  0.0 59.6 %step.1 = (f32[10,40,128]{2,1,0:T(8,128)S(1)}, f32[10,40,128]{2,1,0:T(8,128)S(1)}) custom-call(s32[3,8]{1,0:T(4,128)} %bitcast.8, f32[20,1,1600]{2,1,0:T(1,128)} %bitcast.7, f32[40,1600]{1,0:T(8,128)} %bitcast.6, f32[32,128]{1,0:T(8,128)} %constant.16.clone.rest_0_, f32[64,128]{1,0:T(8,128)} %constant.17.clone.rest_1_, f32[64,32]{1,0:T(8,128)} %constant.18.clone.rest_2_, ...), custom_call_target="tpu_custom_call" | custom-call | tf_op jit(solution)/shard_map/step/pallas_call | solution.py:531
  59.7 2.1 %last.1 = f32[20,1,1600]{2,1,0:T(1,128)} custom-call(f32[10,40,128]{2,1,0:T(8,128)S(1)} %get-tuple-element.7.field, f32[10,40,128]{2,1,0:T(8,128)S(1)} %get-tuple-element.8.coef), custom_call_target="tpu_custom_call" | custom-call | tf_op jit(solution)/shard_map/last/pallas_call | solution.py:554

commit v5 on v4

--- a/solution.py
+++ b/solution.py
@@ -27,8 +27,8 @@
 TABLES = 8
 NEAR = [o for m in range(1, 8) for o in (m, 16 - m)] + [8]
 FAR = NEAR[::-1]
-FIRST_SUM = 12
-SUM_TO = (0, 1, 2, 3, 4, 11, 5, 10, 6, 9, 7, 8, 12, 13, 14, 15)
+SUMS = (13, 14, 15, 0)
+SUM_TO = (0, 1, 2, 3, 4, 5, 6, 11, 7, 10, 8, 9, 12, 13, 14, 15)
 
 
 def wave_list():
@@ -362,18 +362,18 @@
     r2 = jnp.where(left, o_all[0:32], o_all[32:64])
     z_send[...] = r2
 
-    tile_of = zi - FIRST_SUM
-    sums = zi >= FIRST_SUM
+    sums = (zi >= SUMS[0]) | (zi == SUMS[3])
+    tile_of = jnp.where(zi == SUMS[3], 3, zi - SUMS[0])
 
     def z_copy(t, slot):
         return pltpu.make_async_remote_copy(
             src_ref=z_send.at[8 * t : 8 * t + 8], dst_ref=z_recv.at[rows(slot, 8)], send_sem=zs,
-            recv_sem=zr, device_id=at_z(FIRST_SUM + t), device_id_type=MESH,
+            recv_sem=zr, device_id=at_z(SUMS[t]), device_id_type=MESH,
         )
 
     for t in range(4):
 
-        @pl.when(zi != FIRST_SUM + t)
+        @pl.when(zi != SUMS[t])
         def _():
             z_copy(t, zi).start()
 
@@ -396,7 +396,7 @@
 
         whole(z_all.at[0:24], as_, ar).wait_recv()
 
-    @pl.when(zi < FIRST_SUM)
+    @pl.when(jnp.logical_not(sums))
     def _():
         whole(z_all.at[0:32], as_, ar).wait_recv()
 
@@ -457,7 +457,7 @@
         whole(z_send.at[0:24], zs, zr).wait_send()
         whole(z_recv.at[0:120], as_, ar).wait_send()
 
-    @pl.when(zi < FIRST_SUM)
+    @pl.when(jnp.logical_not(sums))
     def _():
         whole(z_send.at[0:32], zs, zr).wait_send()
 

time: 61.9 us -> 61.4 us (level)
  no operation moved by 1% of the time
where the time goes in v5:
time: 61.4 us; the launch traced here: 61.3 us
  Pallas kernels  61.3 us (100%)
    pallas_call x1, Pallas kernels, local(): pl.pallas_call(main_kernel, out_shape=(tile, tile), in_specs=[pl.BlockSpe...  59.2 us
    pallas_call x1, Pallas kernels, local(): pl.pallas_call(last_kernel, out_shape=jax.ShapeDtypeStruct((20, 1, 1600),...  2.07 us

profile of v5, /device:TPU:1, one launch (start us, length us, event | category | flops | bytes accessed | tf_op | source)
XLA Modules:
  0.0 61.3 jit_solution(14337275668369218907)
XLA Ops:
  0.0 59.2 %step.1 = (f32[10,40,128]{2,1,0:T(8,128)S(1)}, f32[10,40,128]{2,1,0:T(8,128)S(1)}) custom-call(s32[3,8]{1,0:T(4,128)} %bitcast.8, f32[20,1,1600]{2,1,0:T(1,128)} %bitcast.7, f32[40,1600]{1,0:T(8,128)} %bitcast.6, f32[32,128]{1,0:T(8,128)} %constant.16.clone.rest_0_, f32[64,128]{1,0:T(8,128)} %constant.17.clone.rest_1_, f32[64,32]{1,0:T(8,128)} %constant.18.clone.rest_2_, ...), custom_call_target="tpu_custom_call" | custom-call | tf_op jit(solution)/shard_map/step/pallas_call | solution.py:531
  59.2 2.1 %last.1 = f32[20,1,1600]{2,1,0:T(1,128)} custom-call(f32[10,40,128]{2,1,0:T(8,128)S(1)} %get-tuple-element.7.field, f32[10,40,128]{2,1,0:T(8,128)S(1)} %get-tuple-element.8.coef), custom_call_target="tpu_custom_call" | custom-call | tf_op jit(solution)/shard_map/last/pallas_call | solution.py:554
